TPU v7x, 128 devices: a whole 4x4x4 slice. The times are simulated.
128 devices in a mesh: side: 2 (over core), shard: 64 (over y, x, z).
Axes of the slice: x: 4, y: 4, z: 4, core: 2. Of those that a mesh axis runs over, the one named last changes fastest.
Arguments:
- sketch: bfloat16 [2, 131072, 128], P('side', 'shard'), may hold values from -6 to 6
- tile_values: bfloat16 [2, 327680, 1024], P('side', 'shard'), may hold values from -100 to 100, as said below
- sent_blocks: int32 [2, 2560], P(None, 'shard'), may hold values from 0 to 15, as said below
- pair_counts: int32 [2, 320], P(None, 'shard'), may hold values from 4 to 8, as said below
Outputs:
- new_sketch: float32 [2, 131072, 128], P('side', 'shard')
Inputs may be any that keep to these rules, and one draw needn't show every extreme that they name: The two sides hold one matrix: tile_values[1, o, j] is the transpose of tile_values[0, (o + j - 2) mod 64, 4 - j] in the layout of the first step. `sent_blocks`: the 8 entries of one side, owner and pair are distinct. `pair_counts`: for every side and owner some pair uses all 8 slots.
All inputs are finite; a program needn't handle non-finite values.
Results may differ from a plain program's by a relative error of at most 0.0003.
Values may be sent and summed in bfloat16 or wider, within the bound.
A program may use at most 64 MiB of HBM per device.

v0:
```python
import jax
import jax.numpy as jnp
from jax import lax
from jax.sharding import PartitionSpec as P

TB = 128
RANK = 128
PEER = 8
HALF = 2
PAIRS = 5


EPSILON = 1e-05


def from_partner(block, axis, stride):
    count = lax.axis_size(axis)
    route = []
    for low in range(count):
        high = low | 1 << stride
        if high != low and high < count:
            route += [(low, high), (high, low)]
    return lax.ppermute(block, axis, route)


def from_behind(x, axis, by):
    length = lax.axis_size(axis)
    return lax.ppermute(x, axis, [(i, (i + by) % length) for i in range(length)])


def select_rows(stacked, position):
    return lax.dynamic_index_in_dim(stacked, position, 0, keepdims=False)


def packed_blocks(source, chosen, live_count):
    picked = source[chosen]
    places = jnp.arange(chosen.shape[1], dtype=jnp.int32)
    usable = places[None, :] < live_count[:, None]
    return jnp.where(usable[:, :, None, None], picked, jnp.zeros_like(picked))


def body(sketch, tile_values, sent_blocks, pair_counts):
    side_pos = lax.axis_index("side")
    block_rows = sketch.shape[1] // TB
    own_sketch = sketch[0].reshape(block_rows, TB, RANK)
    block_lists = sent_blocks.reshape(2, PAIRS, PEER)
    own_lists = select_rows(block_lists, side_pos)
    far_lists = select_rows(block_lists, 1 - side_pos)
    own_counts = select_rows(pair_counts, side_pos)
    far_counts = select_rows(pair_counts, 1 - side_pos)
    facing = from_partner(own_sketch, "side", 0)
    crossed = packed_blocks(facing, far_lists, far_counts)
    offsets = [pair_pos - HALF for pair_pos in range(PAIRS)]
    arrived = [crossed[HALF]] * PAIRS
    for pair_pos in range(PAIRS):
        if offsets[pair_pos] != 0:
            arrived[pair_pos] = from_behind(crossed[pair_pos], "shard", offsets[pair_pos])
    fetched = jnp.stack(arrived[::-1]).reshape(PAIRS, PEER * TB, RANK)
    tile_grid = tile_values[0].reshape(PAIRS, PEER * TB, PEER * TB)
    product = jnp.einsum("jab,jbr->jar", tile_grid, fetched, preferred_element_type=jnp.float32)
    places = jnp.arange(PEER, dtype=jnp.int32)
    usable = places[None, :] < own_counts[:, None]
    targets = jnp.arange(block_rows, dtype=jnp.int32)
    routing = ((own_lists[:, :, None] == targets[None, None, :]) & usable[:, :, None]).astype(
        jnp.float32
    )
    update = jnp.einsum(
        "jak,jatr->ktr",
        routing,
        product.reshape(PAIRS, PEER, TB, RANK),
        precision=lax.Precision.HIGHEST,
    ).reshape(block_rows * TB, RANK)
    partial_value = jnp.einsum("nr,ns->rs", update, update, precision=lax.Precision.HIGHEST)
    summed = lax.psum(partial_value, "shard")
    owners = lax.axis_size("shard")
    gram_matrix = summed / (update.shape[0] * owners) + EPSILON * jnp.eye(RANK, dtype=jnp.float32)
    factor = jnp.linalg.cholesky(gram_matrix)
    result = jax.scipy.linalg.solve_triangular(factor, update.T, lower=True).T
    return result[None]


def solution(mesh):
    return jax.shard_map(
        body,
        mesh=mesh,
        in_specs=(
            P("side", "shard", None),
            P("side", "shard", None),
            P(None, "shard"),
            P(None, "shard"),
        ),
        out_specs=P("side", "shard", None),
        check_vma=False,
    )
```

profile of v0, /device:TPU:0, one launch (start us, length us, event | category | flops | bytes accessed | tf_op | source)
XLA Modules:
  0.0 211.4 jit_solution(3255072321141772111)
XLA Ops:
  6.5 0.0 all-reduce.2.cloned.1.call-start
  6.5 0.0 collective-permute-start
  6.5 0.8 reshape.109
  7.3 0.1 reshape.114
  7.4 0.8 fusion.9
  8.2 0.1 iota_compare_fusion.3
  8.2 0.4 collective-permute-done
  8.7 0.8 gather_fusion
  9.5 0.2 broadcast_select_fusion
  9.6 0.1 slice_bitcast_fusion
  9.8 4.1 %collective-permute-start.1 = (bf16[8,128,128]{2,1,0:T(8,128)(2,1)S(1)}, bf16[8,128,128]{2,1,0:T(8,128)(2,1)S(1)}, u32[]{:S(2)}, u32[]{:S(2)}) collective-permute-start(bf16[8,128,128]{2,1,0:T(8,128)(2,1)S(1)} %get-tuple-element.9), channel_id=1, source_target_pairs={{0,2},{1,3},{2,4},{3,5},{4,6},{5,7},{6,8},{7,9},{8,10},{9,11},{10,... | collective-permute-start | bytes 786440 | tf_op jit(solution)/shard_map/ppermute | solution.py:28
  13.8 1.0 collective-permute-start.2
  14.8 6.4 %collective-permute-start.3 = (bf16[8,128,128]{2,1,0:T(8,128)(2,1)S(1)}, bf16[8,128,128]{2,1,0:T(8,128)(2,1)S(1)}, u32[]{:S(2)}, u32[]{:S(2)}) collective-permute-start(bf16[8,128,128]{2,1,0:T(8,128)(2,1)S(1)} %get-tuple-element.6), channel_id=1, source_target_pairs={{0,63},{1,0},{2,1},{3,2},{4,3},{5,4},{6,5},{7,6},{8,7},{9,8},{10,9... | collective-permute-start | bytes 786440 | tf_op jit(solution)/shard_map/ppermute | solution.py:28
  21.3 0.3 collective-permute-start.4
  21.6 0.1 iota_compare_fusion.4
  21.6 0.1 copy.24
  21.8 3.7 %collective-permute-done.1 = bf16[8,128,128]{2,1,0:T(8,128)(2,1)S(1)} collective-permute-done((bf16[8,128,128]{2,1,0:T(8,128)(2,1)S(1)}, bf16[8,128,128]{2,1,0:T(8,128)(2,1)S(1)}, u32[]{:S(2)}, u32[]{:S(2)}) %collective-permute-start.1) | collective-permute-done | bytes 262176 | tf_op jit(solution)/shard_map/ppermute | solution.py:28
  25.5 0.1 copy.22
  25.6 7.2 %collective-permute-done.2 = bf16[8,128,128]{2,1,0:T(8,128)(2,1)S(1)} collective-permute-done((bf16[8,128,128]{2,1,0:T(8,128)(2,1)S(1)}, bf16[8,128,128]{2,1,0:T(8,128)(2,1)S(1)}, u32[]{:S(2)}, u32[]{:S(2)}) %collective-permute-start.2) | collective-permute-done | bytes 262176 | tf_op jit(solution)/shard_map/ppermute | solution.py:28
  32.8 0.1 copy.23
  32.9 4.0 %collective-permute-done.3 = bf16[8,128,128]{2,1,0:T(8,128)(2,1)S(1)} collective-permute-done((bf16[8,128,128]{2,1,0:T(8,128)(2,1)S(1)}, bf16[8,128,128]{2,1,0:T(8,128)(2,1)S(1)}, u32[]{:S(2)}, u32[]{:S(2)}) %collective-permute-start.3) | collective-permute-done | bytes 262176 | tf_op jit(solution)/shard_map/ppermute | solution.py:28
  36.9 0.1 copy.25
  37.1 0.0 collective-permute-done.4
  37.1 0.1 copy.26
  37.3 7.6 %fusion.11 = f32[5,128,1024]{2,1,0:T(8,128)S(1)} fusion(bf16[5,1024,128]{1,2,0:T(8,128)(2,1)S(1)} %constant_dynamic-update-slice_fusion, bf16[5,1024,1024]{2,1,0:T(8,128)(2,1)} %bitcast.55), kind=kOutput, calls=%fused_computation.40 | convolution fusion | flops 1342177280 | bytes 14417920 | tf_op jit(solution)/shard_map/jab,jbr->jar/dot_general | solution.py:60
  44.9 2.1 %copy.27 = f32[80,8,8,128]{3,2,1,0:T(8,128)} copy(f32[80,8,8,128]{3,1,2,0:T(8,128)S(1)} %bitcast.56) | data formatting | bytes 5242880
  47.1 2.6 %copy.14 = f32[5,8,128,128]{3,1,0,2:T(8,128)S(1)} copy(f32[5,8,128,128]{2,1,3,0:T(8,128)} %bitcast.57) | data formatting | bytes 5242880 | tf_op jit(solution)/shard_map/reshape | solution.py:70
  49.6 1.1 convolution_bitcast_fusion.1
  50.7 0.0 copy-start
  50.7 1.0 copy-done
  51.7 2.5 %convolution_bitcast_fusion.2 = f32[128,128]{1,0:T(8,128)} fusion(f32[16,128,128]{2,0,1:T(8,128)S(1)} %convolution_bitcast_fusion.1), kind=kOutput, calls=%fused_computation.4 | convolution fusion | flops 402653184 | bytes 1114112 | tf_op jit(solution)/shard_map/nr,ns->rs/dot_general | solution.py:73
  54.2 0.0 all-reduce.2.cloned.1.call-update
  54.2 1.6 copy.15
  55.8 122.2 %all-reduce.2.cloned.1.call-done = f32[128,128]{1,0:T(8,128)} async-done(((f32[128,128]{1,0:T(8,128)}), f32[128,128]{1,0:T(8,128)}) %all-reduce.2.cloned.1.call-update) | async-done | bytes 65552 | tf_op jit(solution)/shard_map/psum | solution.py:74
  178.0 0.9 select_add_fusion
  178.8 0.1 copy.18
  178.9 0.9 fusion.2
  179.8 11.7 %cholesky.16 = f32[128,128]{1,0:T(8,128)S(1)} custom-call(f32[128,128]{1,0:T(8,128)S(1)} %fusion.2), custom_call_target="Cholesky" | custom-call | tf_op jit(solution)/shard_map/jit(cholesky)/cholesky | solution.py:77
  191.5 0.6 compare_reduce_fusion
  192.2 0.7 fusion
  192.8 9.8 %custom-call.7 = f32[1,128,128]{1,2,0:T(8,128)S(1)} custom-call(f32[1,128,128]{2,1,0:T(8,128)S(1)} %fusion), custom_call_target="InvertDiagBlocksLowerTriangular" | custom-call | tf_op jit(solution)/shard_map/jit(_solve_triangular)/triangular_solve | solution.py:78
  202.7 1.9 convolution_bitcast_fusion
  (9 shorter events, 0.2 us)
Async XLA Ops:
  6.5 171.4 %all-reduce.2.cloned.1.call-start = ((), (), s32[]{:S(2)}) async-start(), calls=%async_computation | async-start | bytes 131072 | tf_op jit(solution)/shard_map/psum | solution.py:74
  6.5 2.1 %collective-permute-start = (bf16[16,128,128]{2,1,0:T(8,128)(2,1)}, bf16[16,128,128]{2,1,0:T(8,128)(2,1)S(1)}, u32[]{:S(2)}, u32[]{:S(2)}) collective-permute-start(bf16[16,128,128]{2,1,0:T(8,128)(2,1)} %bitcast.65), channel_id=1, source_target_pairs={{0,64},{64,0},{1,65},{65,1},{2,66},{66,2},{3,67},{67,3},{4,68},{68... | collective-permute-start | bytes 1572872 | tf_op jit(solution)/shard_map/ppermute | solution.py:23
  9.8 15.7 %collective-permute-start.1 = (bf16[8,128,128]{2,1,0:T(8,128)(2,1)S(1)}, bf16[8,128,128]{2,1,0:T(8,128)(2,1)S(1)}, u32[]{:S(2)}, u32[]{:S(2)}) collective-permute-start(bf16[8,128,128]{2,1,0:T(8,128)(2,1)S(1)} %get-tuple-element.9), channel_id=1, source_target_pairs={{0,2},{1,3},{2,4},{3,5},{4,6},{5,7},{6,8},{7,9},{8,10},{9,11},{10,... | collective-permute-start | bytes 786440 | tf_op jit(solution)/shard_map/ppermute | solution.py:28
  13.8 19.0 %collective-permute-start.2 = (bf16[8,128,128]{2,1,0:T(8,128)(2,1)S(1)}, bf16[8,128,128]{2,1,0:T(8,128)(2,1)S(1)}, u32[]{:S(2)}, u32[]{:S(2)}) collective-permute-start(bf16[8,128,128]{2,1,0:T(8,128)(2,1)S(1)} %get-tuple-element.8), channel_id=1, source_target_pairs={{0,1},{1,2},{2,3},{3,4},{4,5},{5,6},{6,7},{7,8},{8,9},{9,10},{10,1... | collective-permute-start | bytes 786440 | tf_op jit(solution)/shard_map/ppermute | solution.py:28
  14.8 22.0 %collective-permute-start.3 = (bf16[8,128,128]{2,1,0:T(8,128)(2,1)S(1)}, bf16[8,128,128]{2,1,0:T(8,128)(2,1)S(1)}, u32[]{:S(2)}, u32[]{:S(2)}) collective-permute-start(bf16[8,128,128]{2,1,0:T(8,128)(2,1)S(1)} %get-tuple-element.6), channel_id=1, source_target_pairs={{0,63},{1,0},{2,1},{3,2},{4,3},{5,4},{6,5},{7,6},{8,7},{9,8},{10,9... | collective-permute-start | bytes 786440 | tf_op jit(solution)/shard_map/ppermute | solution.py:28
  21.3 15.8 %collective-permute-start.4 = (bf16[8,128,128]{2,1,0:T(8,128)(2,1)S(1)}, bf16[8,128,128]{2,1,0:T(8,128)(2,1)S(1)}, u32[]{:S(2)}, u32[]{:S(2)}) collective-permute-start(bf16[8,128,128]{2,1,0:T(8,128)(2,1)S(1)} %get-tuple-element.5), channel_id=1, source_target_pairs={{0,62},{1,63},{2,0},{3,1},{4,2},{5,3},{6,4},{7,5},{8,6},{9,7},{10,... | collective-permute-start | bytes 786440 | tf_op jit(solution)/shard_map/ppermute | solution.py:28
  50.7 1.0 copy-start
Sparse Core Ops, SparseCore 0:
  54.4 123.5 all-reduce.1
where the time goes:
time: 212 us; the launch traced here: 211 us
  waiting for transfers between devices  137 us (65%)
  other arithmetic  24.9 us (12%)
  between operations  13.6 us (6%)
  matrix products  13.1 us (6%)
  starting transfers between devices  11.8 us (6%)
  local copies, waits for them, and re-layouts  10.6 us (5%)
    psum x1, waiting for transfers between devices, body(): summed = lax.psum(partial_value, 'shard')  122 us
    ppermute x4, waiting for transfers between devices, from_behind(): lax.ppermute(x, axis, [(i, (i + by) % length) for i in range(length)])  14.8 us
    another operation x3, other arithmetic, body(): factor = jnp.linalg.cholesky(gram_matrix)  12.4 us
    ppermute x4, starting transfers between devices, from_behind(): lax.ppermute(x, axis, [(i, (i + by) % length) for i in range(length)])  11.8 us
    another operation x2, other arithmetic, body(): result = jax.scipy.linalg.solve_triangular(factor, update.T, lower=True).T  10.5 us
    dot_general x1, matrix products, body(): jnp.einsum('jab,jbr->jar', tile_grid, fetched, preferred_element_type=jnp...  7.6 us
  transfers between devices with their start and end apart: 6, of which 5 were waited for; matrix products, arithmetic and copies ran while one was open for 2% of the time, Pallas kernels for 0%

commit v1 on v0

v1 whole, which is shorter than its diff:
```python
import functools

import jax
import jax.numpy as jnp
from jax import lax
from jax.experimental import pallas as pl
from jax.experimental.pallas import tpu as pltpu
from jax.sharding import PartitionSpec as P

TB = 128
RANK = 128
PEER = 8
HALF = 2
PAIRS = 5
BLOCKS = 16
EDGE = PEER * TB
CHUNKS = 4
CROWS = EDGE // CHUNKS
PLANE = 16
EPSILON = 1e-05
F32 = jnp.float32
BF16 = jnp.bfloat16
MESH = pl.DeviceIdType.MESH
HIGHEST = lax.Precision.HIGHEST


def exchange_kernel(
    owners,
    lists_hbm,
    counts_hbm,
    sk_hbm,
    tile_hbm,
    u_hbm,
    gsum,
    lists,
    counts,
    sk,
    tile,
    send,
    recv,
    relay,
    prod,
    u,
    inv,
    gpart,
    rs,
    ybuf,
    in_sem,
    tile_sem,
    a_send,
    a_recv,
    r_send,
    r_recv,
    b_send,
    b_recv,
    rs_send,
    rs_recv,
    y_send,
    y_recv,
    ag_send,
    ag_recv,
):
    side = lax.axis_index("side")
    me = lax.axis_index("shard")
    far = 1 - side
    ahead = lax.rem(me + 1, owners)
    behind = lax.rem(me + owners - 1, owners)
    planes = owners // PLANE
    q = lax.rem(me, PLANE)
    y = me // PLANE
    base = y * PLANE

    inputs = []
    for n, (src, dst) in enumerate(((sk_hbm, sk), (lists_hbm, lists), (counts_hbm, counts))):
        c = pltpu.make_async_copy(src, dst, in_sem.at[n])
        c.start()
        inputs.append(c)
    tile_copies = {}
    for j in (2, 1, 3, 0, 4):
        c = pltpu.make_async_copy(tile_hbm.at[j], tile.at[j], tile_sem.at[j])
        c.start()
        tile_copies[j] = c

    barrier = pltpu.get_barrier_semaphore()
    greet = [(far, ahead), (far, behind), (far, me), (side, ahead), (side, behind)]
    greet += [(side, base + lax.rem(q + i, PLANE)) for i in range(1, PLANE)]
    greet += [(side, lax.rem(me + i * PLANE, owners)) for i in range(1, planes)]
    for d in greet:
        pl.semaphore_signal(barrier, inc=1, device_id=d, device_id_type=MESH)

    for c in inputs:
        c.wait()
    for j in (4, 0, 3, 1, 2):
        live = counts[side, j]

        def pack(b, carry, j=j, live=live):
            block = sk[lists[side, j * PEER + b]]
            keep = jnp.where(b < live, 1.0, 0.0).astype(BF16)
            send[j, pl.ds(pl.multiple_of(b * TB, TB), TB), :] = block * keep
            return carry

        lax.fori_loop(0, PEER, pack, 0)

    pl.semaphore_wait(barrier, len(greet))

    def remote(src, dst, ss, rsem, dev):
        c = pltpu.make_async_remote_copy(
            src_ref=src, dst_ref=dst, send_sem=ss, recv_sem=rsem, device_id=dev, device_id_type=MESH
        )
        return c

    rows = [pl.ds(i * CROWS, CROWS) for i in range(CHUNKS)]
    a_copies = [[], []]
    for i in range(CHUNKS):
        for way, (jj, to) in enumerate(((4, ahead), (0, behind))):
            c = remote(
                send.at[jj, rows[i]], relay.at[way, rows[i]], a_send.at[way, i], a_recv.at[way, i], (far, to)
            )
            c.start()
            a_copies[way].append(c)
    b_copies = {}
    for jj, to in ((2, me), (3, ahead), (1, behind)):
        c = remote(send.at[jj], recv.at[4 - jj], b_send.at[jj], b_recv.at[4 - jj], (far, to))
        c.start()
        b_copies[4 - jj] = c

    def table(n, carry):
        j = n // BLOCKS
        k = lax.rem(n, BLOCKS)
        place = jnp.int32(PEER)
        live = counts[side, j]
        for a in range(PEER):
            hit = jnp.logical_and(lists[side, j * PEER + a] == k, a < live)
            place = jnp.where(hit, jnp.int32(a), place)
        inv[n] = place
        return carry

    lax.fori_loop(0, PAIRS * BLOCKS, table, 0)
    for j in range(PAIRS):
        prod[j, PEER] = jnp.zeros((TB, RANK), F32)

    def multiply(j, k0, depth, first):
        def step(a, carry):
            at = pl.ds(pl.multiple_of(a * 2 * TB, 2 * TB), 2 * TB)
            part = jnp.dot(
                tile[j, at, k0 : k0 + depth], recv[j, k0 : k0 + depth, :], preferred_element_type=F32
            ).reshape(2, TB, RANK)
            where = pl.ds(a * 2, 2)
            if first:
                prod[j, where] = part
            else:
                prod[j, where] = prod[j, where] + part
            return carry

        lax.fori_loop(0, PEER // 2, step, 0)

    b_copies[2].wait_recv()
    tile_copies[2].wait()
    multiply(2, 0, EDGE, True)

    r_copies = [[], []]
    for i in range(CHUNKS):
        for way, (j, to) in enumerate(((0, ahead), (4, behind))):
            a_copies[way][i].wait_recv()
            c = remote(
                relay.at[way, rows[i]], recv.at[j, rows[i]], r_send.at[way, i], r_recv.at[way, i], (side, to)
            )
            c.start()
            r_copies[way].append(c)

    for j in (1, 3):
        b_copies[j].wait_recv()
        tile_copies[j].wait()
        multiply(j, 0, EDGE, True)

    def gather_near(k, carry):
        u[k] = (
            prod[1, inv[BLOCKS + k]] + prod[2, inv[2 * BLOCKS + k]] + prod[3, inv[3 * BLOCKS + k]]
        )
        return carry

    lax.fori_loop(0, BLOCKS, gather_near, 0)

    tile_copies[0].wait()
    tile_copies[4].wait()
    for i in range(CHUNKS):
        for way, j in enumerate((0, 4)):
            r_copies[way][i].wait_recv()
            multiply(j, i * CROWS, CROWS, i == 0)

    gpart[...] = jnp.zeros((RANK, RANK), F32)

    def gather_far(k, carry):
        block = u[k] + prod[0, inv[k]] + prod[4, inv[4 * BLOCKS + k]]
        u[k] = block
        gpart[...] += lax.dot_general(
            block, block, (((0,), (0,)), ((), ())), precision=HIGHEST, preferred_element_type=F32
        )
        return carry

    lax.fori_loop(0, BLOCKS, gather_far, 0)
    u_copy = pltpu.make_async_copy(u, u_hbm, in_sem.at[3])
    u_copy.start()
    rs_copies = []
    for i in range(1, PLANE):
        to = lax.rem(q + i, PLANE)
        c = remote(
            gpart.at[pl.ds(pl.multiple_of(to * 8, 8), 8)],
            rs.at[i],
            rs_send.at[i],
            rs_recv.at[i],
            (side, base + to),
        )
        c.start()
        rs_copies.append(c)
    total = gpart[pl.ds(pl.multiple_of(q * 8, 8), 8), :]
    for i in range(1, PLANE):
        rs_copies[i - 1].wait_recv()
        total = total + rs[i]
    ybuf[0] = total
    y_copies = []
    for i in range(1, planes):
        c = remote(
            ybuf.at[0], ybuf.at[i], y_send.at[i], y_recv.at[i], (side, lax.rem(me + i * PLANE, owners))
        )
        c.start()
        y_copies.append(c)
    for c in y_copies:
        c.wait_recv()
    total = ybuf[0]
    for i in range(1, planes):
        total = total + ybuf[i]
    mine = pl.ds(pl.multiple_of(q * 8, 8), 8)
    gsum[mine, :] = total
    ag_copies = []
    for i in range(1, PLANE):
        to = lax.rem(q + i, PLANE)
        c = remote(gsum.at[mine], gsum.at[mine], ag_send.at[i], ag_recv.at[i], (side, base + to))
        c.start()
        ag_copies.append(c)
    for i in range(1, PLANE):
        src = pl.ds(pl.multiple_of(lax.rem(q + PLANE - i, PLANE) * 8, 8), 8)
        remote(gsum.at[src], gsum.at[src], ag_send.at[i], ag_recv.at[i], (side, me)).wait_recv()

    for group in (a_copies[0], a_copies[1], r_copies[0], r_copies[1], rs_copies, y_copies, ag_copies):
        for c in group:
            c.wait_send()
    for c in b_copies.values():
        c.wait_send()
    u_copy.wait()


def exchange(owners, lists, counts, sketch, tiles):
    dma = pltpu.SemaphoreType.DMA
    vmem = pl.BlockSpec(memory_space=pltpu.VMEM)
    hbm = pl.BlockSpec(memory_space=pl.ANY)
    planes = owners // PLANE
    return pl.pallas_call(
        functools.partial(exchange_kernel, owners),
        name="exchange",
        out_shape=(
            jax.ShapeDtypeStruct((BLOCKS, TB, RANK), F32),
            jax.ShapeDtypeStruct((RANK, RANK), F32),
        ),
        in_specs=[hbm, hbm, hbm, hbm],
        out_specs=(hbm, vmem),
        scratch_shapes=[
            pltpu.SMEM((2, PAIRS * PEER), jnp.int32),
            pltpu.SMEM((2, PAIRS), jnp.int32),
            pltpu.VMEM((BLOCKS, TB, RANK), BF16),
            pltpu.VMEM((PAIRS, EDGE, EDGE), BF16),
            pltpu.VMEM((PAIRS, EDGE, RANK), BF16),
            pltpu.VMEM((PAIRS, EDGE, RANK), BF16),
            pltpu.VMEM((2, EDGE, RANK), BF16),
            pltpu.VMEM((PAIRS, PEER + 1, TB, RANK), F32),
            pltpu.VMEM((BLOCKS, TB, RANK), F32),
            pltpu.SMEM((PAIRS * BLOCKS,), jnp.int32),
            pltpu.VMEM((RANK, RANK), F32),
            pltpu.VMEM((PLANE, 8, RANK), F32),
            pltpu.VMEM((planes, 8, RANK), F32),
            dma((4,)),
            dma((PAIRS,)),
            dma((2, CHUNKS)),
            dma((2, CHUNKS)),
            dma((2, CHUNKS)),
            dma((2, CHUNKS)),
            dma((PAIRS,)),
            dma((PAIRS,)),
            dma((PLANE,)),
            dma((PLANE,)),
            dma((planes,)),
            dma((planes,)),
            dma((PLANE,)),
            dma((PLANE,)),
        ],
        compiler_params=pltpu.CompilerParams(
            collective_id=0, has_side_effects=True, vmem_limit_bytes=67043328
        ),
    )(lists, counts, sketch, tiles)


STEPS = 4


def finish_kernel(rows, g, u_hbm, out_hbm, u, o, am, u_sem, o_sem):
    u_copy = pltpu.make_async_copy(u_hbm, u, u_sem)
    u_copy.start()
    row = lax.broadcasted_iota(jnp.int32, (RANK, RANK), 0)
    col = lax.broadcasted_iota(jnp.int32, (RANK, RANK), 1)
    eye = jnp.where(row == col, 1.0, 0.0).astype(F32)
    am[0] = g[...] * (1.0 / rows) + EPSILON * eye
    am[1] = eye
    sub = lax.broadcasted_iota(jnp.int32, (8, RANK), 0)
    for p in range(RANK // 8):
        lo = 8 * p
        blocks = RANK // 8 - p
        a = [am[0, lo + 8 * t : lo + 8 * t + 8, :] for t in range(blocks)]
        m = [am[1, lo + 8 * t : lo + 8 * t + 8, :] for t in range(blocks)]
        c = [
            [jnp.broadcast_to(a[t][:, lo + j : lo + j + 1], (8, RANK)) for t in range(blocks)]
            for j in range(8)
        ]
        diag = None
        for k in range(8):
            pivot = jnp.broadcast_to(c[k][0][k : k + 1, :], (8, RANK))
            diag = pivot if diag is None else jnp.where(sub == k, pivot, diag)
            recip = 1.0 / pivot
            mult = [c[k][t] * recip for t in range(blocks)]
            mult[0] = jnp.where(sub > k, mult[0], 0.0)
            for j in range(k + 1, 8):
                f = jnp.broadcast_to(c[j][0][k : k + 1, :], (8, RANK))
                for t in range(blocks):
                    c[j][t] = c[j][t] - mult[t] * f
            arow = jnp.broadcast_to(a[0][k : k + 1, :], (8, RANK))
            mrow = jnp.broadcast_to(m[0][k : k + 1, :], (8, RANK))
            for t in range(blocks):
                a[t] = a[t] - mult[t] * arow
                m[t] = m[t] - mult[t] * mrow
        am[1, lo : lo + 8, :] = m[0] * lax.rsqrt(diag)
        for t in range(1, blocks):
            am[0, lo + 8 * t : lo + 8 * t + 8, :] = a[t]
            am[1, lo + 8 * t : lo + 8 * t + 8, :] = m[t]
    u_copy.wait()
    w = am[1]
    step = (BLOCKS * TB) // STEPS
    copies = []
    for s in range(STEPS):
        at = pl.ds(s * step, step)
        o[at, :] = lax.dot_general(
            u[at, :], w, (((1,), (1,)), ((), ())), precision=HIGHEST, preferred_element_type=F32
        )
        c = pltpu.make_async_copy(o.at[at], out_hbm.at[at], o_sem.at[s])
        c.start()
        copies.append(c)
    for c in copies:
        c.wait()


def finish(rows, g, u):
    n = BLOCKS * TB
    return pl.pallas_call(
        functools.partial(finish_kernel, rows),
        name="finish",
        out_shape=jax.ShapeDtypeStruct((n, RANK), F32),
        in_specs=[pl.BlockSpec(memory_space=pltpu.VMEM), pl.BlockSpec(memory_space=pl.ANY)],
        out_specs=pl.BlockSpec(memory_space=pl.ANY),
        scratch_shapes=[
            pltpu.VMEM((n, RANK), F32),
            pltpu.VMEM((n, RANK), F32),
            pltpu.VMEM((2, RANK, RANK), F32),
            pltpu.SemaphoreType.DMA(()),
            pltpu.SemaphoreType.DMA((STEPS,)),
        ],
        compiler_params=pltpu.CompilerParams(vmem_limit_bytes=67043328),
    )(g, u)


def body(sketch, tile_values, sent_blocks, pair_counts):
    owners = lax.axis_size("shard")
    tiles = tile_values[0].reshape(PAIRS, EDGE, EDGE)
    u, g = exchange(owners, sent_blocks, pair_counts, sketch[0].reshape(BLOCKS, TB, RANK), tiles)
    rows = BLOCKS * TB * owners
    return finish(rows, g, u.reshape(BLOCKS * TB, RANK))[None]


def solution(mesh):
    return jax.shard_map(
        body,
        mesh=mesh,
        in_specs=(
            P("side", "shard", None),
            P("side", "shard", None),
            P(None, "shard"),
            P(None, "shard"),
        ),
        out_specs=P("side", "shard", None),
        check_vma=False,
    )
```

time: 212 us -> 57.5 us (0.27)
  waiting for transfers between devices: 137 us -> 0 us
  Pallas kernels: 0 us -> 57.3 us
  other arithmetic: 24.9 us -> 0 us
  between operations: 13.6 us -> 0.01 us
  matrix products: 13.1 us -> 0 us
  starting transfers between devices: 11.8 us -> 0 us
  local copies, waits for them, and re-layouts: 10.6 us -> 0 us
    psum x1 -> x0, waiting for transfers between devices: 122 us -> none  [body(): summed = lax.psum(partial_value, 'shard')]
    pallas_call x0 -> x2, Pallas kernels: none -> 57.3 us  [the longest x1 49.7 us: exchange(): pl.pallas_call(functools.partial(exchange_kernel, owners), name='exchange...]
    another operation x5 -> x0, other arithmetic: 22.9 us -> none  [the longest x3 12.4 us: body(): factor = jnp.linalg.cholesky(gram_matrix)]
    ppermute x5 -> x0, waiting for transfers between devices: 15.2 us -> none  [the longest x4 14.8 us: from_behind(): lax.ppermute(x, axis, [(i, (i + by) % length) for i in range(length)])]
    ppermute x5 -> x0, starting transfers between devices: 11.8 us -> none  [the longest x4 11.8 us: from_behind(): lax.ppermute(x, axis, [(i, (i + by) % length) for i in range(length)])]
    dot_general x3 -> x0, matrix products: 11.2 us -> none  [the longest x1 7.6 us: body(): jnp.einsum('jab,jbr->jar', tile_grid, fetched, preferred_element_type=jnp...]
    reshape x2 -> x0, local copies, waits for them, and re-layouts: 3.31 us -> none  [the longest x1 2.56 us: body(): product.reshape(PAIRS, PEER, TB, RANK)]
    unnamed x7 -> x0, local copies, waits for them, and re-layouts: 3.16 us -> none
  transfers between devices with their start and end apart: 6 -> 0, of which waited for: 5 -> 0; matrix products, arithmetic and copies ran while one was open for 2% -> 0% of each run, Pallas kernels for 0% -> 0%
where the time goes in v1:
time: 57.5 us; the launch traced here: 57.3 us
  Pallas kernels  57.3 us (100%)
    pallas_call x1, Pallas kernels, exchange(): pl.pallas_call(functools.partial(exchange_kernel, owners), name='exchange...  49.7 us
    pallas_call x1, Pallas kernels, finish(): pl.pallas_call(functools.partial(finish_kernel, rows), name='finish', out...  7.54 us

profile of v1, /device:TPU:0, one launch (start us, length us, event | category | flops | bytes accessed | tf_op | source)
XLA Modules:
  0.0 57.3 jit_solution(11919022903932847251)
XLA Ops:
  0.0 49.7 %exchange.1 = (f32[16,128,128]{2,1,0:T(8,128)}, f32[128,128]{1,0:T(8,128)}) custom-call(s32[2,40]{1,0:T(2,128)} %lists_hbm.1, s32[2,5]{1,0:T(2,128)} %counts_hbm.1, bf16[16,128,128]{2,1,0:T(8,128)(2,1)} %bitcast.6, bf16[5,1024,1024]{2,1,0:T(8,128)(2,1)} %bitcast.4), custom_call_target="tpu_custom_call" | custom-call | tf_op jit(solution)/shard_map/exchange/pallas_call | solution.py:258
  49.7 7.5 %finish.1 = f32[2048,128]{1,0:T(8,128)} custom-call(f32[128,128]{1,0:T(8,128)} %get-tuple-element.7.g, f32[2048,128]{1,0:T(8,128)} %bitcast.5), custom_call_target="tpu_custom_call" | custom-call | tf_op jit(solution)/shard_map/finish/pallas_call | solution.py:361

commit v2 on v1

--- a/solution.py
+++ b/solution.py
@@ -16,6 +16,7 @@
 EDGE = PEER * TB
 CHUNKS = 4
 CROWS = EDGE // CHUNKS
+RING = 4
 PLANE = 16
 EPSILON = 1e-05
 F32 = jnp.float32
@@ -24,13 +25,31 @@
 HIGHEST = lax.Precision.HIGHEST
 
 
+def split(x):
+    high = x.astype(BF16)
+    rest = x - high.astype(F32)
+    middle = rest.astype(BF16)
+    return high, middle, (rest - middle.astype(F32)).astype(BF16)
+
+
+def gram(x):
+    def cross(a, b):
+        return lax.dot_general(a, b, (((0,), (0,)), ((), ())), preferred_element_type=F32)
+
+    high, middle, low = split(x)
+    pair = jnp.concatenate([high, middle], 1)
+    both = cross(pair, pair)
+    mixed = both[:RANK, RANK:] + cross(high, low)
+    return both[:RANK, :RANK] + both[RANK:, RANK:] + mixed + mixed.T
+
+
 def exchange_kernel(
     owners,
     lists_hbm,
     counts_hbm,
     sk_hbm,
     tile_hbm,
-    u_hbm,
+    u_parts,
     gsum,
     lists,
     counts,
@@ -59,6 +78,8 @@
     y_recv,
     ag_send,
     ag_recv,
+    plane_sem,
+    hello_sem,
 ):
     side = lax.axis_index("side")
     me = lax.axis_index("shard")
@@ -75,33 +96,43 @@
         c = pltpu.make_async_copy(src, dst, in_sem.at[n])
         c.start()
         inputs.append(c)
-    tile_copies = {}
-    for j in (2, 1, 3, 0, 4):
-        c = pltpu.make_async_copy(tile_hbm.at[j], tile.at[j], tile_sem.at[j])
-        c.start()
-        tile_copies[j] = c
-
+    def signal(sem, device):
+        pl.semaphore_signal(sem, inc=1, device_id=device, device_id_type=MESH)
+
+    ring_z = [(side, me - lax.rem(me, RING) + lax.rem(me + i, RING)) for i in range(1, RING)]
+    ring_x = [(side, base + lax.rem(q + i * RING, PLANE)) for i in range(1, RING)]
+    ring_y = [(side, lax.rem(me + i * PLANE, owners)) for i in range(1, planes)]
+    across = [(far, ahead), (far, behind), (far, me)]
+    greet = [(side, ahead), (side, behind)] + ring_z + ring_x + ring_y
     barrier = pltpu.get_barrier_semaphore()
-    greet = [(far, ahead), (far, behind), (far, me), (side, ahead), (side, behind)]
-    greet += [(side, base + lax.rem(q + i, PLANE)) for i in range(1, PLANE)]
-    greet += [(side, lax.rem(me + i * PLANE, owners)) for i in range(1, planes)]
-    for d in greet:
-        pl.semaphore_signal(barrier, inc=1, device_id=d, device_id_type=MESH)
+    for device in greet:
+        signal(barrier, device)
+
+    @pl.when(side == 0)
+    def _():
+        for device in across:
+            signal(barrier, device)
 
     for c in inputs:
         c.wait()
-    for j in (4, 0, 3, 1, 2):
+
+    def pack(j):
         live = counts[side, j]
-
-        def pack(b, carry, j=j, live=live):
-            block = sk[lists[side, j * PEER + b]]
+        for b in range(PEER):
             keep = jnp.where(b < live, 1.0, 0.0).astype(BF16)
-            send[j, pl.ds(pl.multiple_of(b * TB, TB), TB), :] = block * keep
-            return carry
-
-        lax.fori_loop(0, PEER, pack, 0)
-
-    pl.semaphore_wait(barrier, len(greet))
+            send[j, b * TB : (b + 1) * TB, :] = sk[lists[side, j * PEER + b]] * keep
+
+    for j in (4, 0):
+        pack(j)
+
+    pl.semaphore_wait(barrier, len(greet) + side * len(across))
+    for device in ring_x:
+        signal(plane_sem, device)
+
+    @pl.when(side == 1)
+    def _():
+        for device in across:
+            signal(hello_sem, device)
 
     def remote(src, dst, ss, rsem, dev):
         c = pltpu.make_async_remote_copy(
@@ -114,15 +145,28 @@
     for i in range(CHUNKS):
         for way, (jj, to) in enumerate(((4, ahead), (0, behind))):
             c = remote(
-                send.at[jj, rows[i]], relay.at[way, rows[i]], a_send.at[way, i], a_recv.at[way, i], (far, to)
+                send.at[jj, rows[i]], relay.at[way, rows[i]], a_send.at[way, i], a_recv.at[way, i], (side, to)
             )
             c.start()
             a_copies[way].append(c)
+    for j in (3, 1, 2):
+        pack(j)
+
+    @pl.when(side == 0)
+    def _():
+        pl.semaphore_wait(hello_sem, len(across))
+
     b_copies = {}
     for jj, to in ((2, me), (3, ahead), (1, behind)):
         c = remote(send.at[jj], recv.at[4 - jj], b_send.at[jj], b_recv.at[4 - jj], (far, to))
         c.start()
         b_copies[4 - jj] = c
+
+    tile_copies = {}
+    for j in (2, 1, 3, 0, 4):
+        c = pltpu.make_async_copy(tile_hbm.at[j], tile.at[j], tile_sem.at[j])
+        c.start()
+        tile_copies[j] = c
 
     def table(n, carry):
         j = n // BLOCKS
@@ -163,7 +207,7 @@
         for way, (j, to) in enumerate(((0, ahead), (4, behind))):
             a_copies[way][i].wait_recv()
             c = remote(
-                relay.at[way, rows[i]], recv.at[j, rows[i]], r_send.at[way, i], r_recv.at[way, i], (side, to)
+                relay.at[way, rows[i]], recv.at[j, rows[i]], r_send.at[way, i], r_recv.at[way, i], (far, to)
             )
             c.start()
             r_copies[way].append(c)
@@ -186,21 +230,19 @@
     for i in range(CHUNKS):
         for way, j in enumerate((0, 4)):
             r_copies[way][i].wait_recv()
-            multiply(j, i * CROWS, CROWS, i == 0)
-
-    gpart[...] = jnp.zeros((RANK, RANK), F32)
-
-    def gather_far(k, carry):
-        block = u[k] + prod[0, inv[k]] + prod[4, inv[4 * BLOCKS + k]]
-        u[k] = block
-        gpart[...] += lax.dot_general(
-            block, block, (((0,), (0,)), ((), ())), precision=HIGHEST, preferred_element_type=F32
-        )
-        return carry
-
-    lax.fori_loop(0, BLOCKS, gather_far, 0)
-    u_copy = pltpu.make_async_copy(u, u_hbm, in_sem.at[3])
-    u_copy.start()
+            part = jnp.dot(
+                tile[j, :, i * CROWS : (i + 1) * CROWS], recv[j, rows[i], :], preferred_element_type=F32
+            ).reshape(PEER, TB, RANK)
+            if i == 0:
+                prod[j, 0:PEER] = part
+            else:
+                prod[j, 0:PEER] = prod[j, 0:PEER] + part
+
+    for k in range(BLOCKS):
+        u[k] = u[k] + prod[0, inv[k]] + prod[4, inv[4 * BLOCKS + k]]
+    gpart[...] = gram(u[...].reshape(BLOCKS * TB, RANK))
+
+    pl.semaphore_wait(plane_sem, len(ring_x))
     rs_copies = []
     for i in range(1, PLANE):
         to = lax.rem(q + i, PLANE)
@@ -213,6 +255,13 @@
         )
         c.start()
         rs_copies.append(c)
+    def part(k, carry):
+        at = pl.ds(pl.multiple_of(k * TB, TB), TB)
+        for n, piece in enumerate(split(u[k])):
+            u_parts[at, n * RANK : (n + 1) * RANK] = piece
+        return carry
+
+    lax.fori_loop(0, BLOCKS, part, 0)
     total = gpart[pl.ds(pl.multiple_of(q * 8, 8), 8), :]
     for i in range(1, PLANE):
         rs_copies[i - 1].wait_recv()
@@ -247,7 +296,6 @@
             c.wait_send()
     for c in b_copies.values():
         c.wait_send()
-    u_copy.wait()
 
 
 def exchange(owners, lists, counts, sketch, tiles):
@@ -259,11 +307,11 @@
         functools.partial(exchange_kernel, owners),
         name="exchange",
         out_shape=(
-            jax.ShapeDtypeStruct((BLOCKS, TB, RANK), F32),
-            jax.ShapeDtypeStruct((RANK, RANK), F32),
+            pltpu.VMEM((BLOCKS * TB, 3 * RANK), BF16),
+            pltpu.VMEM((RANK, RANK), F32),
         ),
         in_specs=[hbm, hbm, hbm, hbm],
-        out_specs=(hbm, vmem),
+        out_specs=(vmem, vmem),
         scratch_shapes=[
             pltpu.SMEM((2, PAIRS * PEER), jnp.int32),
             pltpu.SMEM((2, PAIRS), jnp.int32),
@@ -278,7 +326,7 @@
             pltpu.VMEM((RANK, RANK), F32),
             pltpu.VMEM((PLANE, 8, RANK), F32),
             pltpu.VMEM((planes, 8, RANK), F32),
-            dma((4,)),
+            dma((3,)),
             dma((PAIRS,)),
             dma((2, CHUNKS)),
             dma((2, CHUNKS)),
@@ -292,19 +340,23 @@
             dma((planes,)),
             dma((PLANE,)),
             dma((PLANE,)),
+            pltpu.SemaphoreType.REGULAR,
+            pltpu.SemaphoreType.REGULAR,
         ],
         compiler_params=pltpu.CompilerParams(
-            collective_id=0, has_side_effects=True, vmem_limit_bytes=67043328
+            collective_id=0, has_side_effects=True, vmem_limit_bytes=40 * 1024 * 1024
         ),
-    )(lists, counts, sketch, tiles)
+    )(*[pltpu.with_memory_space_constraint(x, pltpu.HBM) for x in (lists, counts, sketch, tiles)])
 
 
 STEPS = 4
 
 
-def finish_kernel(rows, g, u_hbm, out_hbm, u, o, am, u_sem, o_sem):
-    u_copy = pltpu.make_async_copy(u_hbm, u, u_sem)
-    u_copy.start()
+def along(a, b):
+    return lax.dot_general(a, b, (((1,), (1,)), ((), ())), preferred_element_type=F32)
+
+
+def finish_kernel(rows, g, u, out_hbm, o, am, o_sem):
     row = lax.broadcasted_iota(jnp.int32, (RANK, RANK), 0)
     col = lax.broadcasted_iota(jnp.int32, (RANK, RANK), 1)
     eye = jnp.where(row == col, 1.0, 0.0).astype(F32)
@@ -340,15 +392,15 @@
         for t in range(1, blocks):
             am[0, lo + 8 * t : lo + 8 * t + 8, :] = a[t]
             am[1, lo + 8 * t : lo + 8 * t + 8, :] = m[t]
-    u_copy.wait()
-    w = am[1]
+    w0, w1, w2 = split(am[1])
+    near = jnp.concatenate([jnp.concatenate([w0, w1], 1), jnp.concatenate([w1, w0], 1)], 0)
     step = (BLOCKS * TB) // STEPS
     copies = []
     for s in range(STEPS):
         at = pl.ds(s * step, step)
-        o[at, :] = lax.dot_general(
-            u[at, :], w, (((1,), (1,)), ((), ())), precision=HIGHEST, preferred_element_type=F32
-        )
+        both = along(u[at, : 2 * RANK], near)
+        tail = along(u[at, 2 * RANK :], w0) + along(u[at, :RANK], w2)
+        o[at, :] = both[:, :RANK] + (both[:, RANK:] + tail)
         c = pltpu.make_async_copy(o.at[at], out_hbm.at[at], o_sem.at[s])
         c.start()
         copies.append(c)
@@ -362,16 +414,14 @@
         functools.partial(finish_kernel, rows),
         name="finish",
         out_shape=jax.ShapeDtypeStruct((n, RANK), F32),
-        in_specs=[pl.BlockSpec(memory_space=pltpu.VMEM), pl.BlockSpec(memory_space=pl.ANY)],
+        in_specs=[pl.BlockSpec(memory_space=pltpu.VMEM), pl.BlockSpec(memory_space=pltpu.VMEM)],
         out_specs=pl.BlockSpec(memory_space=pl.ANY),
         scratch_shapes=[
             pltpu.VMEM((n, RANK), F32),
-            pltpu.VMEM((n, RANK), F32),
             pltpu.VMEM((2, RANK, RANK), F32),
-            pltpu.SemaphoreType.DMA(()),
             pltpu.SemaphoreType.DMA((STEPS,)),
         ],
-        compiler_params=pltpu.CompilerParams(vmem_limit_bytes=67043328),
+        compiler_params=pltpu.CompilerParams(vmem_limit_bytes=40 * 1024 * 1024),
     )(g, u)
 
 
@@ -380,7 +430,7 @@
     tiles = tile_values[0].reshape(PAIRS, EDGE, EDGE)
     u, g = exchange(owners, sent_blocks, pair_counts, sketch[0].reshape(BLOCKS, TB, RANK), tiles)
     rows = BLOCKS * TB * owners
-    return finish(rows, g, u.reshape(BLOCKS * TB, RANK))[None]
+    return finish(rows, g, u)[None]
 
 
 def solution(mesh):

time: 57.5 us -> 50.1 us (0.87)
  Pallas kernels: 57.3 us -> 50 us
    pallas_call x1, Pallas kernels: 49.7 us -> 44.4 us  [exchange(): pl.pallas_call(functools.partial(exchange_kernel, owners), name='exchange...]
    pallas_call x1, Pallas kernels: 7.54 us -> 5.57 us  [finish(): pl.pallas_call(functools.partial(finish_kernel, rows), name='finish', out...]
where the time goes in v2:
time: 50.1 us; the launch traced here: 50 us
  Pallas kernels  50 us (100%)
    pallas_call x1, Pallas kernels, exchange(): pl.pallas_call(functools.partial(exchange_kernel, owners), name='exchange...  44.4 us
    pallas_call x1, Pallas kernels, finish(): pl.pallas_call(functools.partial(finish_kernel, rows), name='finish', out...  5.57 us

profile of v2, /device:TPU:0, one launch (start us, length us, event | category | flops | bytes accessed | tf_op | source)
XLA Modules:
  0.0 50.0 jit_solution(251541870900811280)
XLA Ops:
  0.0 44.4 %exchange.1 = (bf16[2048,384]{1,0:T(8,128)(2,1)S(1)}, f32[128,128]{1,0:T(8,128)S(1)}) custom-call(s32[2,40]{1,0:T(2,128)} %lists_hbm.1, s32[2,5]{1,0:T(2,128)} %counts_hbm.1, bf16[16,128,128]{2,1,0:T(8,128)(2,1)} %bitcast.4, bf16[5,1024,1024]{2,1,0:T(8,128)(2,1)} %bitcast.3), custom_call_target="tpu_custom_call" | custom-call | tf_op jit(solution)/shard_map/exchange/pallas_call | solution.py:306
  44.4 5.6 %finish.1 = f32[2048,128]{1,0:T(8,128)} custom-call(f32[128,128]{1,0:T(8,128)S(1)} %get-tuple-element.7.g, bf16[2048,384]{1,0:T(8,128)(2,1)S(1)} %get-tuple-element.8.u), custom_call_target="tpu_custom_call" | custom-call | tf_op jit(solution)/shard_map/finish/pallas_call | solution.py:413

commit v3 on v2

--- a/solution.py
+++ b/solution.py
@@ -18,6 +18,9 @@
 CROWS = EDGE // CHUNKS
 RING = 4
 PLANE = 16
+PIECE = 32
+CORNERS = (0, 3, 12, 15)
+EARLY = (0, 1, 4, 2, 5, 8, 3, 6, 9, 12, 7, 10, 13, 11, 14, 15)
 EPSILON = 1e-05
 F32 = jnp.float32
 BF16 = jnp.bfloat16
@@ -243,18 +246,16 @@
     gpart[...] = gram(u[...].reshape(BLOCKS * TB, RANK))
 
     pl.semaphore_wait(plane_sem, len(ring_x))
-    rs_copies = []
-    for i in range(1, PLANE):
-        to = lax.rem(q + i, PLANE)
-        c = remote(
-            gpart.at[pl.ds(pl.multiple_of(to * 8, 8), 8)],
-            rs.at[i],
-            rs_send.at[i],
-            rs_recv.at[i],
-            (side, base + to),
-        )
-        c.start()
-        rs_copies.append(c)
+    def rs_copy(n, at):
+        piece = gpart.at[pl.ds(n * PIECE, PIECE)]
+        return remote(piece, rs.at[at], rs_send.at[n], rs_recv.at[at], (side, base + CORNERS[n]))
+
+    for n, corner in enumerate(CORNERS):
+
+        @pl.when(q != corner)
+        def _(n=n):
+            rs_copy(n, q).start()
+
     def part(k, carry):
         at = pl.ds(pl.multiple_of(k * TB, TB), TB)
         for n, piece in enumerate(split(u[k])):
@@ -262,36 +263,62 @@
         return carry
 
     lax.fori_loop(0, BLOCKS, part, 0)
-    total = gpart[pl.ds(pl.multiple_of(q * 8, 8), 8), :]
-    for i in range(1, PLANE):
-        rs_copies[i - 1].wait_recv()
-        total = total + rs[i]
-    ybuf[0] = total
-    y_copies = []
-    for i in range(1, planes):
-        c = remote(
-            ybuf.at[0], ybuf.at[i], y_send.at[i], y_recv.at[i], (side, lax.rem(me + i * PLANE, owners))
-        )
-        c.start()
-        y_copies.append(c)
-    for c in y_copies:
-        c.wait_recv()
-    total = ybuf[0]
-    for i in range(1, planes):
-        total = total + ybuf[i]
-    mine = pl.ds(pl.multiple_of(q * 8, 8), 8)
-    gsum[mine, :] = total
-    ag_copies = []
-    for i in range(1, PLANE):
-        to = lax.rem(q + i, PLANE)
-        c = remote(gsum.at[mine], gsum.at[mine], ag_send.at[i], ag_recv.at[i], (side, base + to))
-        c.start()
-        ag_copies.append(c)
-    for i in range(1, PLANE):
-        src = pl.ds(pl.multiple_of(lax.rem(q + PLANE - i, PLANE) * 8, 8), 8)
-        remote(gsum.at[src], gsum.at[src], ag_send.at[i], ag_recv.at[i], (side, me)).wait_recv()
-
-    for group in (a_copies[0], a_copies[1], r_copies[0], r_copies[1], rs_copies, y_copies, ag_copies):
+
+    x = q // RING
+    z = lax.rem(q, RING)
+    summing = jnp.logical_and(lax.rem(x, RING - 1) == 0, lax.rem(z, RING - 1) == 0)
+    number = 2 * (x // (RING - 1)) + z // (RING - 1)
+    mine = pl.ds(pl.multiple_of(number * PIECE, PIECE), PIECE)
+
+    def y_copy(i):
+        to = lax.rem(me + i * PLANE, owners)
+        return remote(ybuf.at[y], ybuf.at[y], y_send.at[i], y_recv.at[y], (side, to))
+
+    def ag_copy(to):
+        return remote(gsum.at[mine], gsum.at[mine], ag_send.at[to], ag_recv.at[number], (side, base + to))
+
+    @pl.when(summing)
+    def _():
+        total = gpart[mine, :]
+        for i in range(1, PLANE):
+            src = lax.rem(q + i, PLANE)
+            remote(rs.at[src], rs.at[src], rs_send.at[0], rs_recv.at[src], (side, me)).wait_recv()
+            total = total + rs[src]
+        ybuf[y] = total
+        for i in range(1, planes):
+            y_copy(i).start()
+        for i in range(1, planes):
+            src = lax.rem(y + i, planes)
+            remote(ybuf.at[src], ybuf.at[src], y_send.at[0], y_recv.at[src], (side, me)).wait_recv()
+        total = ybuf[0]
+        for i in range(1, planes):
+            total = total + ybuf[i]
+        gsum[mine, :] = total
+        for to in EARLY:
+
+            @pl.when(q != to)
+            def _(to=to):
+                ag_copy(to).start()
+
+    for n, corner in enumerate(CORNERS):
+
+        @pl.when(q != corner)
+        def _(n=n):
+            piece = gsum.at[pl.ds(n * PIECE, PIECE)]
+            remote(piece, piece, ag_send.at[0], ag_recv.at[n], (side, me)).wait_recv()
+            rs_copy(n, q).wait_send()
+
+    @pl.when(summing)
+    def _():
+        for i in range(1, planes):
+            y_copy(i).wait_send()
+        for to in EARLY:
+
+            @pl.when(q != to)
+            def _(to=to):
+                ag_copy(to).wait_send()
+
+    for group in (a_copies[0], a_copies[1], r_copies[0], r_copies[1]):
         for c in group:
             c.wait_send()
     for c in b_copies.values():
@@ -324,8 +351,8 @@
             pltpu.VMEM((BLOCKS, TB, RANK), F32),
             pltpu.SMEM((PAIRS * BLOCKS,), jnp.int32),
             pltpu.VMEM((RANK, RANK), F32),
-            pltpu.VMEM((PLANE, 8, RANK), F32),
-            pltpu.VMEM((planes, 8, RANK), F32),
+            pltpu.VMEM((PLANE, PIECE, RANK), F32),
+            pltpu.VMEM((planes, PIECE, RANK), F32),
             dma((3,)),
             dma((PAIRS,)),
             dma((2, CHUNKS)),

time: 50.1 us -> 48.5 us (0.968)
  Pallas kernels: 50 us -> 48.4 us
    pallas_call x1, Pallas kernels: 44.4 us -> 42.8 us  [exchange(): pl.pallas_call(functools.partial(exchange_kernel, owners), name='exchange...]
where the time goes in v3:
time: 48.5 us; the launch traced here: 48.4 us
  Pallas kernels  48.4 us (100%)
    pallas_call x1, Pallas kernels, exchange(): pl.pallas_call(functools.partial(exchange_kernel, owners), name='exchange...  42.8 us
    pallas_call x1, Pallas kernels, finish(): pl.pallas_call(functools.partial(finish_kernel, rows), name='finish', out...  5.57 us

profile of v3, /device:TPU:0, one launch (start us, length us, event | category | flops | bytes accessed | tf_op | source)
XLA Modules:
  0.0 48.4 jit_solution(7405060244485493359)
XLA Ops:
  0.0 42.8 %exchange.1 = (bf16[2048,384]{1,0:T(8,128)(2,1)S(1)}, f32[128,128]{1,0:T(8,128)S(1)}) custom-call(s32[2,40]{1,0:T(2,128)} %lists_hbm.1, s32[2,5]{1,0:T(2,128)} %counts_hbm.1, bf16[16,128,128]{2,1,0:T(8,128)(2,1)} %bitcast.4, bf16[5,1024,1024]{2,1,0:T(8,128)(2,1)} %bitcast.3), custom_call_target="tpu_custom_call" | custom-call | tf_op jit(solution)/shard_map/exchange/pallas_call | solution.py:333
  42.8 5.6 %finish.1 = f32[2048,128]{1,0:T(8,128)} custom-call(f32[128,128]{1,0:T(8,128)S(1)} %get-tuple-element.7.g, bf16[2048,384]{1,0:T(8,128)(2,1)S(1)} %get-tuple-element.8.u), custom_call_target="tpu_custom_call" | custom-call | tf_op jit(solution)/shard_map/finish/pallas_call | solution.py:440

commit v4 on v3

--- a/solution.py
+++ b/solution.py
@@ -241,9 +241,13 @@
             else:
                 prod[j, 0:PEER] = prod[j, 0:PEER] + part
 
-    for k in range(BLOCKS):
-        u[k] = u[k] + prod[0, inv[k]] + prod[4, inv[4 * BLOCKS + k]]
-    gpart[...] = gram(u[...].reshape(BLOCKS * TB, RANK))
+    half = BLOCKS // 2
+    sums = []
+    for k0 in (0, half):
+        for k in range(k0, k0 + half):
+            u[k] = u[k] + prod[0, inv[k]] + prod[4, inv[4 * BLOCKS + k]]
+        sums.append(gram(u[k0 : k0 + half].reshape(half * TB, RANK)))
+    gpart[...] = sums[0] + sums[1]
 
     pl.semaphore_wait(plane_sem, len(ring_x))
     def rs_copy(n, at):
@@ -383,6 +387,14 @@
     return lax.dot_general(a, b, (((1,), (1,)), ((), ())), preferred_element_type=F32)
 
 
+def spread(x, k):
+    return jnp.broadcast_to(x[k : k + 1, :], (8, RANK))
+
+
+def fill(x, k):
+    return jnp.broadcast_to(x[:, k : k + 1], (8, RANK))
+
+
 def finish_kernel(rows, g, u, out_hbm, o, am, o_sem):
     row = lax.broadcasted_iota(jnp.int32, (RANK, RANK), 0)
     col = lax.broadcasted_iota(jnp.int32, (RANK, RANK), 1)
@@ -390,28 +402,33 @@
     am[0] = g[...] * (1.0 / rows) + EPSILON * eye
     am[1] = eye
     sub = lax.broadcasted_iota(jnp.int32, (8, RANK), 0)
+    ahead = None
     for p in range(RANK // 8):
         lo = 8 * p
         blocks = RANK // 8 - p
         a = [am[0, lo + 8 * t : lo + 8 * t + 8, :] for t in range(blocks)]
         m = [am[1, lo + 8 * t : lo + 8 * t + 8, :] for t in range(blocks)]
-        c = [
-            [jnp.broadcast_to(a[t][:, lo + j : lo + j + 1], (8, RANK)) for t in range(blocks)]
-            for j in range(8)
-        ]
-        diag = None
+        c = [[fill(a[t], lo + j) for t in range(blocks)] for j in range(8)]
+        if ahead is not None:
+            for j in range(8):
+                c[j][0] = ahead[j]
+        ahead = [fill(a[1], lo + 8 + j) for j in range(8)] if blocks > 1 else None
+        diag = jnp.zeros((8, RANK), F32)
         for k in range(8):
-            pivot = jnp.broadcast_to(c[k][0][k : k + 1, :], (8, RANK))
-            diag = pivot if diag is None else jnp.where(sub == k, pivot, diag)
+            pivot = spread(c[k][0], k)
+            diag = jnp.where(sub == k, pivot, diag)
             recip = 1.0 / pivot
             mult = [c[k][t] * recip for t in range(blocks)]
             mult[0] = jnp.where(sub > k, mult[0], 0.0)
             for j in range(k + 1, 8):
-                f = jnp.broadcast_to(c[j][0][k : k + 1, :], (8, RANK))
+                f = spread(c[j][0], k)
                 for t in range(blocks):
                     c[j][t] = c[j][t] - mult[t] * f
-            arow = jnp.broadcast_to(a[0][k : k + 1, :], (8, RANK))
-            mrow = jnp.broadcast_to(m[0][k : k + 1, :], (8, RANK))
+            if ahead is not None:
+                for j in range(8):
+                    ahead[j] = ahead[j] - mult[1] * spread(c[k][1], j)
+            arow = spread(a[0], k)
+            mrow = spread(m[0], k)
             for t in range(blocks):
                 a[t] = a[t] - mult[t] * arow
                 m[t] = m[t] - mult[t] * mrow

time: 48.5 us -> 48.2 us (level)
  no operation moved by 1% of the time
where the time goes in v4:
time: 48.2 us; the launch traced here: 48.1 us
  Pallas kernels  48.1 us (100%)
    pallas_call x1, Pallas kernels, exchange(): pl.pallas_call(functools.partial(exchange_kernel, owners), name='exchange...  42.7 us
    pallas_call x1, Pallas kernels, finish(): pl.pallas_call(functools.partial(finish_kernel, rows), name='finish', out...  5.41 us

profile of v4, /device:TPU:0, one launch (start us, length us, event | category | flops | bytes accessed | tf_op | source)
XLA Modules:
  0.0 48.1 jit_solution(5547966670291864162)
XLA Ops:
  0.0 42.7 %exchange.1 = (bf16[2048,384]{1,0:T(8,128)(2,1)S(1)}, f32[128,128]{1,0:T(8,128)S(1)}) custom-call(s32[2,40]{1,0:T(2,128)} %lists_hbm.1, s32[2,5]{1,0:T(2,128)} %counts_hbm.1, bf16[16,128,128]{2,1,0:T(8,128)(2,1)} %bitcast.4, bf16[5,1024,1024]{2,1,0:T(8,128)(2,1)} %bitcast.3), custom_call_target="tpu_custom_call" | custom-call | tf_op jit(solution)/shard_map/exchange/pallas_call | solution.py:337
  42.7 5.4 %finish.1 = f32[2048,128]{1,0:T(8,128)} custom-call(f32[128,128]{1,0:T(8,128)S(1)} %get-tuple-element.7.g, bf16[2048,384]{1,0:T(8,128)(2,1)S(1)} %get-tuple-element.8.u), custom_call_target="tpu_custom_call" | custom-call | tf_op jit(solution)/shard_map/finish/pallas_call | solution.py:457

commit v5 on v4

--- a/solution.py
+++ b/solution.py
@@ -240,12 +240,15 @@
                 prod[j, 0:PEER] = part
             else:
                 prod[j, 0:PEER] = prod[j, 0:PEER] + part
+            if i == CHUNKS - 1 and way == 0:
+                for k in range(BLOCKS):
+                    u[k] = u[k] + prod[0, inv[k]]
 
     half = BLOCKS // 2
     sums = []
     for k0 in (0, half):
         for k in range(k0, k0 + half):
-            u[k] = u[k] + prod[0, inv[k]] + prod[4, inv[4 * BLOCKS + k]]
+            u[k] = u[k] + prod[4, inv[4 * BLOCKS + k]]
         sums.append(gram(u[k0 : k0 + half].reshape(half * TB, RANK)))
     gpart[...] = sums[0] + sums[1]
 

time: 48.2 us -> 48.4 us (level)
  no operation moved by 1% of the time
where the time goes in v5:
time: 48.4 us; the launch traced here: 48.2 us
  Pallas kernels  48.2 us (100%)
    pallas_call x1, Pallas kernels, exchange(): pl.pallas_call(functools.partial(exchange_kernel, owners), name='exchange...  42.8 us
    pallas_call x1, Pallas kernels, finish(): pl.pallas_call(functools.partial(finish_kernel, rows), name='finish', out...  5.41 us

profile of v5, /device:TPU:0, one launch (start us, length us, event | category | flops | bytes accessed | tf_op | source)
XLA Modules:
  0.0 48.2 jit_solution(18347797420945470093)
XLA Ops:
  0.0 42.8 %exchange.1 = (bf16[2048,384]{1,0:T(8,128)(2,1)S(1)}, f32[128,128]{1,0:T(8,128)S(1)}) custom-call(s32[2,40]{1,0:T(2,128)} %lists_hbm.1, s32[2,5]{1,0:T(2,128)} %counts_hbm.1, bf16[16,128,128]{2,1,0:T(8,128)(2,1)} %bitcast.4, bf16[5,1024,1024]{2,1,0:T(8,128)(2,1)} %bitcast.3), custom_call_target="tpu_custom_call" | custom-call | tf_op jit(solution)/shard_map/exchange/pallas_call | solution.py:340
  42.8 5.4 %finish.1 = f32[2048,128]{1,0:T(8,128)} custom-call(f32[128,128]{1,0:T(8,128)S(1)} %get-tuple-element.7.g, bf16[2048,384]{1,0:T(8,128)(2,1)S(1)} %get-tuple-element.8.u), custom_call_target="tpu_custom_call" | custom-call | tf_op jit(solution)/shard_map/finish/pallas_call | solution.py:460
